TPU v7x, 32 devices: a whole 2x2x4 slice. The times are simulated.
32 devices in a mesh: dp: 8 (over y, x, core), mp: 4 (over z).
Axes of the slice: x: 2, y: 2, z: 4, core: 2. Of those that a mesh axis runs over, the one named last changes fastest.
Arguments:
- series: bfloat16 [8, 512, 16, 256], P('dp', 'mp'), may hold values from -6 to 6
- upstream_grad: bfloat16 [8, 512, 16, 256], P('dp', None, 'mp'), may hold values from -3 to 3
- time_weights: bfloat16 [4, 256, 256], replicated, may hold values from -0.375 to 0.375
- channel_weights: bfloat16 [4, 256, 256], replicated, may hold values from -0.375 to 0.375
- neighbors: int32 [4, 3], replicated, may hold values from 0 to 3, as said below
Outputs:
- mixed_series: bfloat16 [8, 512, 16, 256], P('dp', None, 'mp')
- series_grad: bfloat16 [8, 512, 16, 256], P('dp', 'mp')
- time_grads: float32 [4, 256, 256], P(None, 'mp')
- channel_grads: float32 [4, 256, 256], P(None, 'mp')
Inputs may be any that keep to these rules, and one draw needn't show every extreme that they name: `neighbors`: row b names 3 different blocks; its first entry is b.
All inputs are finite; a program needn't handle non-finite values.
Results may differ from a plain program's by a relative error of at most 0.025.
Values may be sent and summed in bfloat16 or wider, within the bound.
A program may use at most 192 MiB of HBM per device.

v0:
```python
import functools

import jax
import jax.numpy as jnp
from jax import lax
from jax.experimental import pallas as pl
from jax.experimental.pallas import tpu as pltpu
from jax.sharding import PartitionSpec as P

HEADS = 4
EPS = 1e-06
LOGIT_SCALE = 0.25
GROUP = 128

F32 = jnp.float32
BF16 = jnp.bfloat16


def mm(a, b):
    return lax.dot_general(a, b, (((1,), (0,)), ((), ())), preferred_element_type=F32)


def mm_nt(a, b):
    return lax.dot_general(a, b, (((1,), (1,)), ((), ())), preferred_element_type=F32)


def mm_tn(a, b):
    return lax.dot_general(a, b, (((0,), (0,)), ((), ())), preferred_element_type=F32)


def head_blocks(features):
    width = features // HEADS
    rows = lax.broadcasted_iota(jnp.int32, (features, features), 0) // width
    cols = lax.broadcasted_iota(jnp.int32, (features, features), 1) // width
    return jnp.where(rows == cols, 1.0 / width, 0.0).astype(BF16)


def head_mean(values, blocks):
    high = values.astype(BF16)
    low = (values - high.astype(F32)).astype(BF16)
    return mm(high, blocks) + mm(low, blocks)


def inv_rms(values):
    return lax.rsqrt(jnp.mean(values * values, axis=-1, keepdims=True) + EPS)


def head_hat(raw, blocks):
    inv = lax.rsqrt(head_mean(raw * raw, blocks) + EPS)
    return raw * inv, inv


def head_back(raw, grad, blocks):
    hat, inv = head_hat(raw, blocks)
    return inv * (grad - hat * head_mean(hat * grad, blocks))


def row_back(rows, grad):
    inv = inv_rms(rows)
    hat = rows * inv
    return inv * (grad - hat * jnp.mean(hat * grad, axis=-1, keepdims=True))


def head_of_lane(shape):
    return lax.broadcasted_iota(jnp.int32, shape, 1) // (shape[1] // HEADS)


def stack_heads(rows):
    lane_head = head_of_lane(rows.shape)
    wide = rows.astype(F32)
    return jnp.concatenate(
        [jnp.where(lane_head == h, wide, 0.0).astype(BF16) for h in range(HEADS)], axis=0
    )


def pick_heads(stacked):
    count = stacked.shape[0] // HEADS
    lane_head = head_of_lane((count, stacked.shape[1]))
    out = stacked[:count]
    for h in range(1, HEADS):
        out = jnp.where(lane_head == h, stacked[h * count : (h + 1) * count], out)
    return out


def softmax_rows(q_stack, keys, keep):
    exponent = jnp.exp(LOGIT_SCALE * mm_nt(q_stack, keys))
    if keep is not None:
        exponent = exponent * keep
    return exponent * (1.0 / jnp.sum(exponent, axis=-1, keepdims=True))


def score_grads(attention, g_stack, values):
    grad = mm_nt(g_stack, values)
    delta = jnp.sum(attention * grad, axis=-1, keepdims=True)
    return (LOGIT_SCALE * attention * (grad - delta)).astype(BF16)


def same_channel(length):
    shape = (HEADS * GROUP, GROUP)
    rows = lax.rem(lax.broadcasted_iota(jnp.int32, shape, 0), GROUP) // length
    cols = lax.broadcasted_iota(jnp.int32, shape, 1) // length
    return jnp.where(rows == cols, 1.0, 0.0).astype(F32)


def project(normed, w_ref, blocks):
    raw_query = mm(normed, w_ref[0])
    raw_key = mm(normed, w_ref[1])
    value = mm(normed, w_ref[2]).astype(BF16)
    query = head_hat(raw_query, blocks)[0].astype(BF16)
    key = head_hat(raw_key, blocks)[0].astype(BF16)
    return raw_query, raw_key, query, key, value


def time_forward_kernel(length, x_ref, w_ref, out_ref, mixed_s, rows_s):
    rows = x_ref.shape[0]
    blocks = head_blocks(x_ref.shape[1])
    keep = same_channel(length)
    x = x_ref[...].astype(F32)
    normed = (x * inv_rms(x)).astype(BF16)
    _, _, query, key, value = project(normed, w_ref, blocks)
    for start in range(0, rows, GROUP):
        sl = slice(start, start + GROUP)
        weights = softmax_rows(stack_heads(query[sl]), key[sl], keep).astype(BF16)
        mixed_s[sl, :] = pick_heads(mm(weights, value[sl])).astype(BF16)
    stream = x + mm(mixed_s[...], w_ref[3])
    count = rows // length
    half = x_ref.shape[1] // 2
    for part in range(2):
        rows_s[part] = stream[:, part * half : (part + 1) * half]
    for seg in range(length):
        for part in range(2):
            out_ref[seg, :, part * half : (part + 1) * half] = rows_s[
                part, pl.ds(seg, count, stride=length), :
            ].astype(BF16)


def time_backward_kernel(
    length, x_ref, sg_ref, w_ref, out_ref, wg_ref, mixed_s, dq_s, dk_s, dv_s, rows_s
):
    rows, features = x_ref.shape
    count = rows // length
    half = features // 2
    blocks = head_blocks(features)
    keep = same_channel(length)
    for seg in range(length):
        for part in range(2):
            rows_s[part, pl.ds(seg, count, stride=length), :] = sg_ref[
                seg, :, part * half : (part + 1) * half
            ].astype(F32)
    up = jnp.concatenate([rows_s[0], rows_s[1]], axis=1)
    up_b = up.astype(BF16)
    x = x_ref[...].astype(F32)
    normed = (x * inv_rms(x)).astype(BF16)
    raw_query, raw_key, query, key, value = project(normed, w_ref, blocks)
    mixed_grad = mm_nt(up_b, w_ref[3]).astype(BF16)
    for start in range(0, rows, GROUP):
        sl = slice(start, start + GROUP)
        q_stack = stack_heads(query[sl])
        g_stack = stack_heads(mixed_grad[sl])
        attention = softmax_rows(q_stack, key[sl], keep)
        weights = attention.astype(BF16)
        mixed_s[sl, :] = pick_heads(mm(weights, value[sl])).astype(BF16)
        grads = score_grads(attention, g_stack, value[sl])
        dq_s[sl, :] = pick_heads(mm(grads, key[sl]))
        dk_s[sl, :] = mm_tn(grads, q_stack)
        dv_s[sl, :] = mm_tn(weights, g_stack)
    finish_backward(
        x, up, up_b, normed, raw_query, raw_key, mixed_s, dq_s, dk_s, dv_s, w_ref, wg_ref, blocks,
        out_ref,
    )


def finish_backward(
    x, up, up_b, normed, raw_query, raw_key, mixed_s, dq_s, dk_s, dv_s, w_ref, wg_ref, blocks, out_ref
):
    query_back = head_back(raw_query, dq_s[...], blocks).astype(BF16)
    key_back = head_back(raw_key, dk_s[...], blocks).astype(BF16)
    value_back = dv_s[...].astype(BF16)

    @pl.when(pl.program_id(0) == 0)
    def _():
        wg_ref[...] = jnp.zeros_like(wg_ref)

    wg_ref[0] += mm_tn(normed, query_back)
    wg_ref[1] += mm_tn(normed, key_back)
    wg_ref[2] += mm_tn(normed, value_back)
    wg_ref[3] += mm_tn(mixed_s[...], up_b)
    grad = mm_nt(query_back, w_ref[0]) + mm_nt(key_back, w_ref[1]) + mm_nt(value_back, w_ref[2])
    result = (up + row_back(x, grad)).astype(BF16)
    out_ref[...] = result.reshape(out_ref.shape)


def channel_kernel(
    near, nbr_ref, x_ref, up_ref, w_ref, out_ref, sg_ref, wg_ref,
    q_s, k_s, v_s, g_s, mixed_s, dq_s, dk_s, dv_s,
):
    channels, features = q_s.shape
    block = channels // nbr_ref.shape[0]
    blocks = head_blocks(features)
    x = x_ref[...].reshape(channels, features).astype(F32)
    normed = (x * inv_rms(x)).astype(BF16)
    raw_query, raw_key, query, key, value = project(normed, w_ref, blocks)
    q_s[...] = query
    k_s[...] = key
    v_s[...] = value
    up_b = up_ref[...].reshape(channels, features)
    g_s[...] = mm_nt(up_b, w_ref[3]).astype(BF16)
    dk_s[...] = jnp.zeros_like(dk_s)
    dv_s[...] = jnp.zeros_like(dv_s)

    def one_block(i, carry):
        mine = pl.ds(pl.multiple_of(i * block, block), block)
        theirs = [
            pl.ds(pl.multiple_of(nbr_ref[i, n] * block, block), block) for n in range(near)
        ]
        q_stack = stack_heads(q_s[mine, :])
        g_stack = stack_heads(g_s[mine, :])
        keys = jnp.concatenate([k_s[t, :] for t in theirs], axis=0)
        values = jnp.concatenate([v_s[t, :] for t in theirs], axis=0)
        attention = softmax_rows(q_stack, keys, None)
        weights = attention.astype(BF16)
        mixed_s[mine, :] = pick_heads(mm(weights, values)).astype(BF16)
        grads = score_grads(attention, g_stack, values)
        dq_s[mine, :] = pick_heads(mm(grads, keys))
        key_grad = mm_tn(grads, q_stack)
        value_grad = mm_tn(weights, g_stack)
        for n, t in enumerate(theirs):
            dk_s[t, :] += key_grad[n * block : (n + 1) * block]
            dv_s[t, :] += value_grad[n * block : (n + 1) * block]
        return carry

    lax.fori_loop(0, nbr_ref.shape[0], one_block, 0)
    out_ref[...] = (x + mm(mixed_s[...], w_ref[3])).astype(BF16).reshape(out_ref.shape)
    finish_backward(
        x, up_b.astype(F32), up_b, normed, raw_query, raw_key, mixed_s, dq_s, dk_s, dv_s, w_ref,
        wg_ref, blocks, sg_ref,
    )


VMEM_LIMIT = 56 * 1024 * 1024


def forward_time(rows, weights, length, step):
    total, features = rows.shape
    count = step // length
    return pl.pallas_call(
        functools.partial(time_forward_kernel, length),
        out_shape=jax.ShapeDtypeStruct((length, total // length, features), BF16),
        grid=(total // step,),
        in_specs=[
            pl.BlockSpec((step, features), lambda i: (i, 0)),
            pl.BlockSpec(weights.shape, lambda i: (0, 0, 0)),
        ],
        out_specs=pl.BlockSpec((length, count, features), lambda i: (0, i, 0)),
        scratch_shapes=[
            pltpu.VMEM((step, features), BF16),
            pltpu.VMEM((2, step, features // 2), F32),
        ],
        compiler_params=pltpu.CompilerParams(vmem_limit_bytes=VMEM_LIMIT),
        name="time_forward",
    )(rows, weights)


def backward_time(rows, grads, weights, length, step):
    total, features = rows.shape
    count = step // length
    return pl.pallas_call(
        functools.partial(time_backward_kernel, length),
        out_shape=(
            jax.ShapeDtypeStruct((total, features), BF16),
            jax.ShapeDtypeStruct(weights.shape, F32),
        ),
        grid=(total // step,),
        in_specs=[
            pl.BlockSpec((step, features), lambda i: (i, 0)),
            pl.BlockSpec((length, count, features), lambda i: (0, i, 0)),
            pl.BlockSpec(weights.shape, lambda i: (0, 0, 0)),
        ],
        out_specs=(
            pl.BlockSpec((step, features), lambda i: (i, 0)),
            pl.BlockSpec(weights.shape, lambda i: (0, 0, 0)),
        ),
        scratch_shapes=[pltpu.VMEM((step, features), BF16)]
        + [pltpu.VMEM((step, features), F32)] * 3
        + [pltpu.VMEM((2, step, features // 2), F32)],
        compiler_params=pltpu.CompilerParams(vmem_limit_bytes=VMEM_LIMIT),
        name="time_backward",
    )(rows, grads, weights)


def channel_layer(columns, upstream, weights, neighbors):
    parts, segments, own, features = columns.shape
    channels = parts * own
    seg_block = pl.BlockSpec((parts, 1, own, features), lambda i: (0, i, 0, 0))
    row_block = pl.BlockSpec((1, channels, features), lambda i: (i, 0, 0))
    w_block = pl.BlockSpec(weights.shape, lambda i: (0, 0, 0))
    return pl.pallas_call(
        functools.partial(channel_kernel, neighbors.shape[1]),
        out_shape=(
            jax.ShapeDtypeStruct(upstream.shape, BF16),
            jax.ShapeDtypeStruct(columns.shape, BF16),
            jax.ShapeDtypeStruct(weights.shape, F32),
        ),
        grid=(segments,),
        in_specs=[pl.BlockSpec(memory_space=pltpu.SMEM), seg_block, row_block, w_block],
        out_specs=(row_block, seg_block, w_block),
        scratch_shapes=[pltpu.VMEM((channels, features), BF16)] * 5
        + [pltpu.VMEM((channels, features), F32)] * 3,
        compiler_params=pltpu.CompilerParams(vmem_limit_bytes=VMEM_LIMIT),
        name="channel_layer",
    )(neighbors, columns, upstream, weights)


def reduce_grads(partial_sum):
    mine = lax.psum_scatter(partial_sum.astype(BF16), "mp", scatter_dimension=1, tiled=True)
    return lax.psum(mine, "dp").astype(F32)


def shards(series, upstream_grad, time_weights, channel_weights, neighbors):
    model_size = lax.axis_size("mp")
    data_size = lax.axis_size("dp")
    own, length, features = series.shape[1:]
    seg_count = length // model_size
    rows = series.reshape(own * length, features)
    step = min(own * length, 512)
    upstream = jnp.swapaxes(upstream_grad[0], 0, 1)
    stream = forward_time(rows, time_weights, length, step)
    columns = lax.all_to_all(
        stream.reshape(model_size, seg_count, own, features), "mp", split_axis=0, concat_axis=0
    )
    output, stream_grad, channel_part = channel_layer(columns, upstream, channel_weights, neighbors)
    returned = lax.all_to_all(stream_grad, "mp", split_axis=0, concat_axis=0)
    channel_grads = reduce_grads(channel_part) / data_size
    series_grad, time_part = backward_time(
        rows, returned.reshape(length, own, features), time_weights, length, step
    )
    time_grads = reduce_grads(time_part) / data_size
    return (
        jnp.swapaxes(output, 0, 1)[None],
        series_grad.reshape(series.shape),
        time_grads,
        channel_grads,
    )


def solution(mesh):
    placed = (P("dp", "mp", None, None), P("dp", None, "mp", None), P(), P(), P())
    return jax.shard_map(
        shards,
        mesh=mesh,
        in_specs=placed,
        out_specs=(
            P("dp", None, "mp", None),
            P("dp", "mp", None, None),
            P(None, "mp", None),
            P(None, "mp", None),
        ),
        check_vma=False,
    )
```

profile of v0, /device:TPU:0, one launch (start us, length us, event | category | flops | bytes accessed | tf_op | source)
XLA Modules:
  0.0 229.5 jit_solution(12247484864105802661)
XLA Ops:
  7.2 9.0 %time_forward.1 = bf16[16,128,256]{2,1,0:T(8,128)(2,1)} custom-call(bf16[2048,256]{1,0:T(8,128)(2,1)} %bitcast.12, bf16[4,256,256]{2,1,0:T(8,128)(2,1)} %w_ref.5), custom_call_target="tpu_custom_call" | custom-call | tf_op jit(solution)/shard_map/time_forward/pallas_call | solution.py:246
  16.2 6.5 %all-to-all-start = ((bf16[4,4,128,256]{3,2,1,0:T(8,128)(2,1)}), bf16[4,4,128,256]{3,2,1,0:T(8,128)(2,1)S(1)}, u32[]{:S(2)}, u32[]{:S(2)}) async-start(bf16[4,4,128,256]{3,2,1,0:T(8,128)(2,1)} %bitcast.16), calls=%async_computation | async-start | bytes 2097152 | tf_op jit(solution)/shard_map/all_to_all | solution.py:328
  22.7 0.0 copy-done.3
  22.7 1.1 copy.12
  23.8 24.6 %all-to-all-done.x_ref = bf16[4,4,128,256]{3,2,1,0:T(8,128)(2,1)S(1)} async-done(((bf16[4,4,128,256]{3,2,1,0:T(8,128)(2,1)}), bf16[4,4,128,256]{3,2,1,0:T(8,128)(2,1)S(1)}, u32[]{:S(2)}, u32[]{:S(2)}) %all-to-all-start) | async-done | bytes 1048608 | tf_op jit(solution)/shard_map/all_to_all | solution.py:328
  48.4 1.0 copy-done.1
  49.4 35.3 %channel_layer.1 = (bf16[4,512,256]{2,1,0:T(8,128)(2,1)}, bf16[4,4,128,256]{3,2,1,0:T(8,128)(2,1)}, f32[4,256,256]{2,1,0:T(8,128)}) custom-call(s32[4,3]{1,0:T(4,128)} %nbr_ref.1, bf16[4,4,128,256]{3,2,1,0:T(8,128)(2,1)} %copy-done.1, bf16[4,512,256]{2,1,0:T(8,128)(2,1)} %bitcast.15, bf16[4,256,256]{2,1,0:T(8,128)(2,1)} %w_ref.4), custom_call_target="tpu_custom_call" | custom-call | tf_op jit(solution)/shard_map/channel_layer/pallas_call | solution.py:297
  84.6 3.7 %all-to-all-start.1 = ((bf16[4,4,128,256]{3,2,1,0:T(8,128)(2,1)}), bf16[4,4,128,256]{3,2,1,0:T(8,128)(2,1)S(1)}, u32[]{:S(2)}, u32[]{:S(2)}) async-start(bf16[4,4,128,256]{3,2,1,0:T(8,128)(2,1)} %get-tuple-element.10), calls=%async_computation.1 | async-start | bytes 2097152 | tf_op jit(solution)/shard_map/all_to_all | solution.py:332
  88.3 0.0 reduce-scatter.5.cloned.1.call-start
  88.4 0.9 convert_element_type.14
  89.2 0.0 reduce-scatter.5.cloned.1.call-update
  89.2 0.0 reduce-scatter.3.cloned.1.call-start
  89.3 32.7 %all-to-all-done.1 = bf16[4,4,128,256]{3,2,1,0:T(8,128)(2,1)S(1)} async-done(((bf16[4,4,128,256]{3,2,1,0:T(8,128)(2,1)}), bf16[4,4,128,256]{3,2,1,0:T(8,128)(2,1)S(1)}, u32[]{:S(2)}, u32[]{:S(2)}) %all-to-all-start.1) | async-done | bytes 1048608 | tf_op jit(solution)/shard_map/all_to_all | solution.py:332
  122.0 1.0 copy-done
  123.0 19.6 %time_backward.1 = (bf16[2048,256]{1,0:T(8,128)(2,1)}, f32[4,256,256]{2,1,0:T(8,128)}) custom-call(bf16[2048,256]{1,0:T(8,128)(2,1)} %bitcast.13, bf16[16,128,256]{2,1,0:T(8,128)(2,1)} %bitcast.14, bf16[4,256,256]{2,1,0:T(8,128)(2,1)} %w_ref.5), custom_call_target="tpu_custom_call" | custom-call | tf_op jit(solution)/shard_map/time_backward/pallas_call | solution.py:267
  142.6 2.2 convert_element_type.12
  144.7 0.0 reduce-scatter.3.cloned.1.call-update
  144.7 0.0 all-reduce.3.cloned.1.call-start
  144.8 0.0 reduce-scatter.5.cloned.1.call-done
  144.8 21.0 %reduce-scatter.3.cloned.1.call-done = bf16[4,64,256]{2,1,0:T(8,128)(2,1)} async-done(((bf16[4,256,256]{2,1,0:T(8,128)(2,1)}), bf16[4,64,256]{2,1,0:T(8,128)(2,1)}) %reduce-scatter.3.cloned.1.call-update) | async-done | bytes 131088 | tf_op jit(solution)/shard_map/reduce_scatter | solution.py:315
  165.8 0.0 all-reduce.3.cloned.1.call-update
  165.9 1.8 copy.10
  167.7 53.5 %all-reduce.3.cloned.1.call-done = (bf16[4,64,256]{2,1,0:T(8,128)(2,1)}, bf16[4,64,256]{2,1,0:T(8,128)(2,1)}) async-done(((bf16[4,64,256]{2,1,0:T(8,128)(2,1)}, bf16[4,64,256]{2,1,0:T(8,128)(2,1)}), (bf16[4,64,256]{2,1,0:T(8,128)(2,1)}, bf16[4,64,256]{2,1,0:T(8,128)(2,1)})) %all-reduce.3.cloned.1.call-update) | async-done | bytes 262160 | tf_op jit(solution)/shard_map/psum | solution.py:316
  221.2 1.8 convert_multiply_fusion
  (7 shorter events, 0.0 us)
Async XLA Ops:
  16.2 6.5 %copy-start.3 = (bf16[1,512,4,256]{3,2,1,0:T(4,128)(2,1)S(1)}, bf16[1,512,4,256]{3,2,1,0:T(4,128)(2,1)}, u32[]{:S(2)}) copy-start(bf16[1,512,4,256]{3,2,1,0:T(4,128)(2,1)} %param.6) | copy-start | bytes 3145732
  16.2 32.2 %all-to-all-start = ((bf16[4,4,128,256]{3,2,1,0:T(8,128)(2,1)}), bf16[4,4,128,256]{3,2,1,0:T(8,128)(2,1)S(1)}, u32[]{:S(2)}, u32[]{:S(2)}) async-start(bf16[4,4,128,256]{3,2,1,0:T(8,128)(2,1)} %bitcast.16), calls=%async_computation | async-start | bytes 2097152 | tf_op jit(solution)/shard_map/all_to_all | solution.py:328
  48.4 1.0 copy-start.1
  84.6 3.7 %copy-start.2 = (f32[4,256,256]{2,1,0:T(8,128)S(1)}, f32[4,256,256]{2,1,0:T(8,128)}, u32[]{:S(2)}) copy-start(f32[4,256,256]{2,1,0:T(8,128)} %get-tuple-element.13) | copy-start | bytes 3145732
  84.6 37.3 %all-to-all-start.1 = ((bf16[4,4,128,256]{3,2,1,0:T(8,128)(2,1)}), bf16[4,4,128,256]{3,2,1,0:T(8,128)(2,1)S(1)}, u32[]{:S(2)}, u32[]{:S(2)}) async-start(bf16[4,4,128,256]{3,2,1,0:T(8,128)(2,1)} %get-tuple-element.10), calls=%async_computation.1 | async-start | bytes 2097152 | tf_op jit(solution)/shard_map/all_to_all | solution.py:332
  88.3 56.5 %reduce-scatter.5.cloned.1.call-start = ((), (), s32[]{:S(2)}) async-start(), calls=%async_computation.5 | async-start | bytes 655360 | tf_op jit(solution)/shard_map/reduce_scatter | solution.py:315
  89.2 76.6 %reduce-scatter.3.cloned.1.call-start = ((), (), s32[]{:S(2)}) async-start(), calls=%async_computation.4 | async-start | bytes 655360 | tf_op jit(solution)/shard_map/reduce_scatter | solution.py:315
  122.0 1.0 copy-start
  142.5 23.3 %copy-start.4 = (bf16[4,512,256]{2,1,0:T(8,128)(2,1)S(1)}, bf16[4,512,256]{2,1,0:T(8,128)(2,1)}, u32[]{:S(2)}) copy-start(bf16[4,512,256]{2,1,0:T(8,128)(2,1)} %get-tuple-element.9) | copy-start | bytes 3145732
  144.7 76.5 %all-reduce.3.cloned.1.call-start = ((), (), s32[]{:S(2)}) async-start(), calls=%async_computation.6 | async-start | bytes 524288 | tf_op jit(solution)/shard_map/psum | solution.py:316
Sparse Core Ops, SparseCore 0:
  91.4 28.8 reduce-scatter.4
  144.9 20.9 reduce-scatter.2
  168.9 52.2 all-reduce.2
where the time goes:
time: 230 us
  waiting for transfers between devices  132 us (57%)
  Pallas kernels  63.9 us (28%)
  between operations  13.8 us (6%)
  starting transfers between devices  10.3 us (4%)
  local copies, waits for them, and re-layouts  4.84 us (2%)
  other arithmetic  4.81 us (2%)
    psum x1, waiting for transfers between devices, reduce_grads(): return lax.psum(mine, 'dp').astype(F32)  53.5 us
    pallas_call x1, Pallas kernels, channel_layer(): pl.pallas_call(functools.partial(channel_kernel, neighbors.shape[1]), out...  35.3 us
    all_to_all x1, waiting for transfers between devices, shards(): returned = lax.all_to_all(stream_grad, 'mp', split_axis=0, concat_axis=0)  32.7 us
    all_to_all x1, waiting for transfers between devices, shards(): lax.all_to_all(stream.reshape(model_size, seg_count, own, features), 'mp'...  24.6 us
    reduce_scatter x2, waiting for transfers between devices, reduce_grads(): lax.psum_scatter(partial_sum.astype(BF16), 'mp', scatter_dimension=1, til...  21.1 us
    pallas_call x1, Pallas kernels, backward_time(): pl.pallas_call(functools.partial(time_backward_kernel, length), out_shape...  19.6 us
    pallas_call x1, Pallas kernels, forward_time(): pl.pallas_call(functools.partial(time_forward_kernel, length), out_shape=...  9.03 us
    all_to_all x1, starting transfers between devices, shards(): lax.all_to_all(stream.reshape(model_size, seg_count, own, features), 'mp'...  6.48 us
  transfers between devices with their start and end apart: 5, of which 4 were waited for; matrix products, arithmetic and copies ran while one was open for 3% of the time, Pallas kernels for 9%

commit v1 on v0

--- a/solution.py
+++ b/solution.py
@@ -14,6 +14,7 @@
 
 F32 = jnp.float32
 BF16 = jnp.bfloat16
+MESH = pl.DeviceIdType.MESH
 
 
 def mm(a, b):
@@ -164,77 +165,192 @@
         dq_s[sl, :] = pick_heads(mm(grads, key[sl]))
         dk_s[sl, :] = mm_tn(grads, q_stack)
         dv_s[sl, :] = mm_tn(weights, g_stack)
-    finish_backward(
-        x, up, up_b, normed, raw_query, raw_key, mixed_s, dq_s, dk_s, dv_s, w_ref, wg_ref, blocks,
-        out_ref,
+
+    @pl.when(pl.program_id(0) == 0)
+    def _():
+        wg_ref[...] = jnp.zeros_like(wg_ref)
+
+    out_ref[...] = finish_backward(
+        x, up, up_b, normed, raw_query, raw_key, mixed_s[...], dq_s, dk_s, dv_s, w_ref, wg_ref, blocks
     )
 
 
 def finish_backward(
-    x, up, up_b, normed, raw_query, raw_key, mixed_s, dq_s, dk_s, dv_s, w_ref, wg_ref, blocks, out_ref
+    x, up, up_b, normed, raw_query, raw_key, mixed, dq_s, dk_s, dv_s, w_ref, wg_ref, blocks
 ):
     query_back = head_back(raw_query, dq_s[...], blocks).astype(BF16)
     key_back = head_back(raw_key, dk_s[...], blocks).astype(BF16)
     value_back = dv_s[...].astype(BF16)
-
-    @pl.when(pl.program_id(0) == 0)
-    def _():
-        wg_ref[...] = jnp.zeros_like(wg_ref)
-
     wg_ref[0] += mm_tn(normed, query_back)
     wg_ref[1] += mm_tn(normed, key_back)
     wg_ref[2] += mm_tn(normed, value_back)
-    wg_ref[3] += mm_tn(mixed_s[...], up_b)
+    wg_ref[3] += mm_tn(mixed, up_b)
     grad = mm_nt(query_back, w_ref[0]) + mm_nt(key_back, w_ref[1]) + mm_nt(value_back, w_ref[2])
-    result = (up + row_back(x, grad)).astype(BF16)
-    out_ref[...] = result.reshape(out_ref.shape)
+    return (up + row_back(x, grad)).astype(BF16)
+
+
+def greet(peers):
+    barrier = pltpu.get_barrier_semaphore()
+    for peer in peers:
+        pl.semaphore_signal(barrier, inc=1, device_id=peer, device_id_type=MESH)
+    pl.semaphore_wait(barrier, len(peers))
+
+
+def others(axis, size):
+    me = lax.axis_index(axis)
+    return [lax.rem(me + k, size) for k in range(1, size)]
 
 
 def channel_kernel(
-    near, nbr_ref, x_ref, up_ref, w_ref, out_ref, sg_ref, wg_ref,
-    q_s, k_s, v_s, g_s, mixed_s, dq_s, dk_s, dv_s,
+    parts, keep_ref, stream_ref, up_ref, w_ref, out_ref, ret_ref, wg_ref,
+    cols_s, sg_s, q_s, k_s, v_s, g_s, mixed_s, dq_s, dk_s, dv_s,
+    in_send, in_recv, back_send, back_recv, own_sem,
 ):
-    channels, features = q_s.shape
-    block = channels // nbr_ref.shape[0]
+    segments, channels, features = up_ref.shape
+    block_count = keep_ref.shape[0]
+    block = channels // block_count
     blocks = head_blocks(features)
-    x = x_ref[...].reshape(channels, features).astype(F32)
-    normed = (x * inv_rms(x)).astype(BF16)
-    raw_query, raw_key, query, key, value = project(normed, w_ref, blocks)
-    q_s[...] = query
-    k_s[...] = key
-    v_s[...] = value
-    up_b = up_ref[...].reshape(channels, features)
-    g_s[...] = mm_nt(up_b, w_ref[3]).astype(BF16)
-    dk_s[...] = jnp.zeros_like(dk_s)
-    dv_s[...] = jnp.zeros_like(dv_s)
-
-    def one_block(i, carry):
-        mine = pl.ds(pl.multiple_of(i * block, block), block)
-        theirs = [
-            pl.ds(pl.multiple_of(nbr_ref[i, n] * block, block), block) for n in range(near)
-        ]
-        q_stack = stack_heads(q_s[mine, :])
-        g_stack = stack_heads(g_s[mine, :])
-        keys = jnp.concatenate([k_s[t, :] for t in theirs], axis=0)
-        values = jnp.concatenate([v_s[t, :] for t in theirs], axis=0)
-        attention = softmax_rows(q_stack, keys, None)
-        weights = attention.astype(BF16)
-        mixed_s[mine, :] = pick_heads(mm(weights, values)).astype(BF16)
-        grads = score_grads(attention, g_stack, values)
-        dq_s[mine, :] = pick_heads(mm(grads, keys))
-        key_grad = mm_tn(grads, q_stack)
-        value_grad = mm_tn(weights, g_stack)
-        for n, t in enumerate(theirs):
-            dk_s[t, :] += key_grad[n * block : (n + 1) * block]
-            dv_s[t, :] += value_grad[n * block : (n + 1) * block]
+    me = lax.axis_index("mp")
+    peers = others("mp", parts)
+    greet([{"mp": peer} for peer in peers])
+
+    def inward(k, seg):
+        return pltpu.make_async_remote_copy(
+            src_ref=stream_ref.at[peers[k], seg],
+            dst_ref=cols_s.at[me, seg],
+            send_sem=in_send.at[k, seg],
+            recv_sem=in_recv.at[k, seg],
+            device_id={"mp": peers[k]},
+            device_id_type=MESH,
+        )
+
+    def back(k, seg):
+        return pltpu.make_async_remote_copy(
+            src_ref=sg_s.at[peers[k], seg],
+            dst_ref=ret_ref.at[me, seg],
+            send_sem=back_send.at[k, seg],
+            recv_sem=back_recv.at[k, seg],
+            device_id={"mp": peers[k]},
+            device_id_type=MESH,
+        )
+
+    def keep_own(seg):
+        return pltpu.make_async_copy(sg_s.at[me, seg], ret_ref.at[me, seg], own_sem.at[seg])
+
+    for seg in range(segments):
+        for k in range(parts - 1):
+            inward(k, seg).start()
+    cols_s[me] = stream_ref[me]
+    wg_ref[...] = jnp.zeros_like(wg_ref)
+
+    def one_segment(seg, carry):
+        up_b = up_ref[seg]
+        g_s[...] = mm_nt(up_b, w_ref[3]).astype(BF16)
+        for k in range(parts - 1):
+            inward(k, seg).wait_recv()
+        x = cols_s[:, seg].reshape(channels, features).astype(F32)
+        normed = (x * inv_rms(x)).astype(BF16)
+        raw_query, raw_key, query, key, value = project(normed, w_ref, blocks)
+        q_s[...] = query
+        k_s[...] = key
+        v_s[...] = value
+
+        dk_s[...] = jnp.zeros_like(dk_s)
+        dv_s[...] = jnp.zeros_like(dv_s)
+
+        def one_block(i, inner):
+            mine = pl.ds(pl.multiple_of(i * block, block), block)
+            q_stack = stack_heads(q_s[mine, :])
+            g_stack = stack_heads(g_s[mine, :])
+            attention = softmax_rows(q_stack, k_s[...], keep_ref[i])
+            weights = attention.astype(BF16)
+            mixed_s[mine, :] = pick_heads(mm(weights, v_s[...])).astype(BF16)
+            grads = score_grads(attention, g_stack, v_s[...])
+            dq_s[mine, :] = pick_heads(mm(grads, k_s[...]))
+            dk_s[...] += mm_tn(grads, q_stack)
+            dv_s[...] += mm_tn(weights, g_stack)
+            return inner
+
+        lax.fori_loop(0, block_count, one_block, 0)
+        sg = finish_backward(
+            x, up_b.astype(F32), up_b, normed, raw_query, raw_key, mixed_s[...], dq_s, dk_s, dv_s,
+            w_ref, wg_ref, blocks,
+        )
+        sg_s[:, seg] = sg.reshape(parts, channels // parts, features)
+        for k in range(parts - 1):
+            back(k, seg).start()
+        keep_own(seg).start()
+        out_ref[seg] = (x + mm(mixed_s[...], w_ref[3])).astype(BF16)
         return carry
 
-    lax.fori_loop(0, nbr_ref.shape[0], one_block, 0)
-    out_ref[...] = (x + mm(mixed_s[...], w_ref[3])).astype(BF16).reshape(out_ref.shape)
-    finish_backward(
-        x, up_b.astype(F32), up_b, normed, raw_query, raw_key, mixed_s, dq_s, dk_s, dv_s, w_ref,
-        wg_ref, blocks, sg_ref,
-    )
+    lax.fori_loop(0, segments, one_segment, 0)
+    for seg in range(segments):
+        keep_own(seg).wait()
+        for k in range(parts - 1):
+            inward(k, seg).wait_send()
+            back(k, seg).wait()
+
+
+def reduce_kernel(
+    dp, mp, time_ref, chan_ref, time_out, chan_out, all_s, dp_in, mp_mine, mp_in, done_s, done_in,
+    send1, recv1, send2, recv2, send3, recv3,
+):
+    matrices = time_ref.shape[0]
+    width = all_s.shape[2]
+    splits = time_ref.shape[2] // width
+    me_dp, me_mp = lax.axis_index("dp"), lax.axis_index("mp")
+    dp_peers, mp_peers = others("dp", dp), others("mp", mp)
+    greet([{"dp": peer} for peer in dp_peers] + [{"mp": peer} for peer in mp_peers])
+
+    def exchange(src, dst, send, recv, k, device):
+        return pltpu.make_async_remote_copy(
+            src_ref=src, dst_ref=dst, send_sem=send.at[k], recv_sem=recv.at[k],
+            device_id=device, device_id_type=MESH,
+        )
+
+    for source, ref in enumerate((time_ref, chan_ref)):
+        for m in range(matrices):
+            for part in range(splits):
+                place = (source * matrices + m) * splits + part
+                all_s[place] = ref[m, :, part * width : (part + 1) * width].astype(BF16)
+    copies = [
+        exchange(all_s.at[p], dp_in.at[k], send1, recv1, k, {"dp": p})
+        for k, p in enumerate(dp_peers)
+    ]
+    for copy in copies:
+        copy.start()
+    for copy in copies:
+        copy.wait()
+    total = all_s[me_dp].astype(F32)
+    for k in range(dp - 1):
+        total = total + dp_in[k].astype(F32)
+    mp_mine[...] = total.astype(BF16).reshape(mp_mine.shape)
+    copies = [
+        exchange(mp_mine.at[p], mp_in.at[k], send2, recv2, k, {"mp": p})
+        for k, p in enumerate(mp_peers)
+    ]
+    for copy in copies:
+        copy.start()
+    for copy in copies:
+        copy.wait()
+    total = mp_mine[me_mp].astype(F32)
+    for k in range(mp - 1):
+        total = total + mp_in[k].astype(F32)
+    done_s[...] = total.astype(BF16)
+    copies = [
+        exchange(done_s, done_in.at[me_dp], send3, recv3, k, {"dp": p})
+        for k, p in enumerate(dp_peers)
+    ]
+    for copy in copies:
+        copy.start()
+    done_in[me_dp] = done_s[...]
+    for copy in copies:
+        copy.wait()
+    for source, ref in enumerate((time_out, chan_out)):
+        for m in range(matrices):
+            for part in range(splits):
+                place = (source * matrices + m) * splits + part
+                ref[m, :, part * width : (part + 1) * width] = done_in[place].astype(F32) / dp
 
 
 VMEM_LIMIT = 56 * 1024 * 1024
@@ -288,53 +404,82 @@
     )(rows, grads, weights)
 
 
-def channel_layer(columns, upstream, weights, neighbors):
-    parts, segments, own, features = columns.shape
+def channel_layer(stream, upstream, weights, neighbors):
+    parts, segments, own, features = stream.shape
     channels = parts * own
-    seg_block = pl.BlockSpec((parts, 1, own, features), lambda i: (0, i, 0, 0))
-    row_block = pl.BlockSpec((1, channels, features), lambda i: (i, 0, 0))
-    w_block = pl.BlockSpec(weights.shape, lambda i: (0, 0, 0))
+    block_count = neighbors.shape[0]
+    lane_block = jnp.arange(channels, dtype=jnp.int32) // (channels // block_count)
+    keep = jnp.any(neighbors[:, :, None] == lane_block[None, None, :], axis=1, keepdims=True)
+    vmem = pl.BlockSpec(memory_space=pltpu.VMEM)
+    rows_b = pltpu.VMEM((channels, features), BF16)
+    rows_f = pltpu.VMEM((channels, features), F32)
+    pair_sems = pltpu.SemaphoreType.DMA((parts - 1, segments))
     return pl.pallas_call(
-        functools.partial(channel_kernel, neighbors.shape[1]),
+        functools.partial(channel_kernel, parts),
         out_shape=(
             jax.ShapeDtypeStruct(upstream.shape, BF16),
-            jax.ShapeDtypeStruct(columns.shape, BF16),
+            jax.ShapeDtypeStruct(stream.shape, BF16),
             jax.ShapeDtypeStruct(weights.shape, F32),
         ),
-        grid=(segments,),
-        in_specs=[pl.BlockSpec(memory_space=pltpu.SMEM), seg_block, row_block, w_block],
-        out_specs=(row_block, seg_block, w_block),
-        scratch_shapes=[pltpu.VMEM((channels, features), BF16)] * 5
-        + [pltpu.VMEM((channels, features), F32)] * 3,
-        compiler_params=pltpu.CompilerParams(vmem_limit_bytes=VMEM_LIMIT),
+        in_specs=[vmem] * 4,
+        out_specs=(vmem, pl.BlockSpec(memory_space=pl.ANY), vmem),
+        scratch_shapes=[pltpu.VMEM(stream.shape, BF16)] * 2
+        + [rows_b] * 5
+        + [rows_f] * 3
+        + [pair_sems] * 4
+        + [pltpu.SemaphoreType.DMA((segments,))],
+        compiler_params=pltpu.CompilerParams(
+            vmem_limit_bytes=VMEM_LIMIT, collective_id=0, has_side_effects=True
+        ),
         name="channel_layer",
-    )(neighbors, columns, upstream, weights)
-
-
-def reduce_grads(partial_sum):
-    mine = lax.psum_scatter(partial_sum.astype(BF16), "mp", scatter_dimension=1, tiled=True)
-    return lax.psum(mine, "dp").astype(F32)
+    )(keep.astype(F32), stream, upstream, weights)
+
+
+def reduce_grads(time_part, channel_part):
+    dp, mp = lax.axis_size("dp"), lax.axis_size("mp")
+    matrices, rows, features = time_part.shape
+    width = features * 2 * matrices // dp
+    mine = rows // mp
+    vmem = pl.BlockSpec(memory_space=pltpu.VMEM)
+    out = jax.ShapeDtypeStruct((matrices, mine, features), F32)
+    return pl.pallas_call(
+        functools.partial(reduce_kernel, dp, mp),
+        out_shape=(out, out),
+        in_specs=[vmem, vmem],
+        out_specs=(vmem, vmem),
+        scratch_shapes=[
+            pltpu.VMEM((dp, rows, width), BF16),
+            pltpu.VMEM((dp - 1, rows, width), BF16),
+            pltpu.VMEM((mp, mine, width), BF16),
+            pltpu.VMEM((mp - 1, mine, width), BF16),
+            pltpu.VMEM((mine, width), BF16),
+            pltpu.VMEM((dp, mine, width), BF16),
+        ]
+        + [pltpu.SemaphoreType.DMA((dp - 1,))] * 2
+        + [pltpu.SemaphoreType.DMA((mp - 1,))] * 2
+        + [pltpu.SemaphoreType.DMA((dp - 1,))] * 2,
+        compiler_params=pltpu.CompilerParams(
+            vmem_limit_bytes=VMEM_LIMIT, collective_id=1, has_side_effects=True
+        ),
+        name="reduce_grads",
+    )(time_part, channel_part)
 
 
 def shards(series, upstream_grad, time_weights, channel_weights, neighbors):
     model_size = lax.axis_size("mp")
-    data_size = lax.axis_size("dp")
     own, length, features = series.shape[1:]
     seg_count = length // model_size
     rows = series.reshape(own * length, features)
     step = min(own * length, 512)
     upstream = jnp.swapaxes(upstream_grad[0], 0, 1)
     stream = forward_time(rows, time_weights, length, step)
-    columns = lax.all_to_all(
-        stream.reshape(model_size, seg_count, own, features), "mp", split_axis=0, concat_axis=0
+    output, returned, channel_part = channel_layer(
+        stream.reshape(model_size, seg_count, own, features), upstream, channel_weights, neighbors
     )
-    output, stream_grad, channel_part = channel_layer(columns, upstream, channel_weights, neighbors)
-    returned = lax.all_to_all(stream_grad, "mp", split_axis=0, concat_axis=0)
-    channel_grads = reduce_grads(channel_part) / data_size
     series_grad, time_part = backward_time(
         rows, returned.reshape(length, own, features), time_weights, length, step
     )
-    time_grads = reduce_grads(time_part) / data_size
+    time_grads, channel_grads = reduce_grads(time_part, channel_part)
     return (
         jnp.swapaxes(output, 0, 1)[None],
         series_grad.reshape(series.shape),

time: 230 us -> 121 us (0.53)
  waiting for transfers between devices: 132 us -> 0 us
  Pallas kernels: 63.9 us -> 112 us
  between operations: 13.8 us -> 0.66 us
  starting transfers between devices: 10.3 us -> 0 us
  other arithmetic: 4.81 us -> 0.1 us
  local copies, waits for them, and re-layouts: 4.84 us -> 7.91 us
    all_to_all x2 -> x0, waiting for transfers between devices: 57.3 us -> none  [the longest x1 32.7 us: shards(): returned = lax.all_to_all(stream_grad, 'mp', split_axis=0, concat_axis=0)]
    psum x1 -> x0, waiting for transfers between devices: 53.5 us -> none  [reduce_grads(): return lax.psum(mine, 'dp').astype(F32)]
    pallas_call x1 -> x2, Pallas kernels: 35.3 us -> 82.4 us  [the longest x1 55.6 us: channel_layer(): pl.pallas_call(functools.partial(channel_kernel, parts), out_shape=(jax.S...]
    reduce_scatter x2 -> x0, waiting for transfers between devices: 21.1 us -> none  [reduce_grads(): lax.psum_scatter(partial_sum.astype(BF16), 'mp', scatter_dimension=1, til...]
    all_to_all x2 -> x0, starting transfers between devices: 10.1 us -> none  [the longest x1 6.48 us: shards(): lax.all_to_all(stream.reshape(model_size, seg_count, own, features), 'mp'...]
    convert_element_type x2 -> x1, other arithmetic: 3.01 us -> 0.01 us  [channel_layer(): keep.astype(F32)]
    unnamed x12 -> x9, local copies, waits for them, and re-layouts: 4.84 us -> 7.31 us
  transfers between devices with their start and end apart: 5 -> 0, of which waited for: 4 -> 0; matrix products, arithmetic and copies ran while one was open for 3% -> 0% of each run, Pallas kernels for 9% -> 0%
where the time goes in v1:
time: 121 us; the launch traced here: 120 us
  Pallas kernels  112 us (93%)
  local copies, waits for them, and re-layouts  7.91 us (7%)
    pallas_call x1, Pallas kernels, channel_layer(): pl.pallas_call(functools.partial(channel_kernel, parts), out_shape=(jax.S...  55.6 us
    pallas_call x1, Pallas kernels, reduce_grads(): pl.pallas_call(functools.partial(reduce_kernel, dp, mp), out_shape=(out,...  26.8 us
    pallas_call x1, Pallas kernels, backward_time(): pl.pallas_call(functools.partial(time_backward_kernel, length), out_shape...  20 us
    pallas_call x1, Pallas kernels, forward_time(): pl.pallas_call(functools.partial(time_forward_kernel, length), out_shape=...  9.1 us
    unnamed x9, local copies, waits for them, and re-layouts  7.31 us

profile of v1, /device:TPU:0, one launch (start us, length us, event | category | flops | bytes accessed | tf_op | source)
XLA Modules:
  0.0 120.2 jit_solution(11247496125116574739)
XLA Ops:
  0.6 0.8 copy.11
  1.4 0.1 compare_reduce_fusion
  1.5 0.6 reshape.48.keep_ref
  2.1 0.0 copy-start
  2.1 9.1 %time_forward.1 = bf16[16,128,256]{2,1,0:T(8,128)(2,1)} custom-call(bf16[2048,256]{1,0:T(8,128)(2,1)} %bitcast.12, bf16[4,256,256]{2,1,0:T(8,128)(2,1)} %w_ref.5), custom_call_target="tpu_custom_call" | custom-call | tf_op jit(solution)/shard_map/time_forward/pallas_call | solution.py:362
  11.2 0.0 copy-done
  11.2 1.1 copy.15
  12.3 55.6 %channel_layer.1 = (bf16[4,512,256]{2,1,0:T(8,128)(2,1)}, bf16[4,4,128,256]{3,2,1,0:T(8,128)(2,1)}, f32[4,256,256]{2,1,0:T(8,128)}) custom-call(f32[4,1,512]{2,1,0:T(1,128)} %reshape.48.keep_ref, bf16[4,4,128,256]{3,2,1,0:T(8,128)(2,1)} %bitcast.14, bf16[4,512,256]{2,1,0:T(8,128)(2,1)} %bitcast.15, bf16[4,256,256]{2,1,0:T(8,128)(2,1)} %w_ref.4), custom_call_target="tpu_custom_call" | custom-call | tf_op jit(solution)/shard_map/channel_layer/pallas_call | solution.py:417
  67.9 3.0 %copy.13 = bf16[1,512,4,256]{3,2,1,0:T(4,128)(2,1)} copy(bf16[1,512,4,256]{3,1,2,0:T(8,128)(2,1)} %bitcast.17) | data formatting | bytes 2097152
  70.9 20.0 %time_backward.1 = (bf16[2048,256]{1,0:T(8,128)(2,1)}, f32[4,256,256]{2,1,0:T(8,128)}) custom-call(bf16[2048,256]{1,0:T(8,128)(2,1)} %bitcast.13, bf16[16,128,256]{2,1,0:T(8,128)(2,1)} %bitcast.16, bf16[4,256,256]{2,1,0:T(8,128)(2,1)} %w_ref.5), custom_call_target="tpu_custom_call" | custom-call | tf_op jit(solution)/shard_map/time_backward/pallas_call | solution.py:383
  91.0 26.8 %reduce_grads.1 = (f32[4,64,256]{2,1,0:T(8,128)}, f32[4,64,256]{2,1,0:T(8,128)}) custom-call(f32[4,256,256]{2,1,0:T(8,128)} %get-tuple-element.14.time_ref, f32[4,256,256]{2,1,0:T(8,128)} %get-tuple-element.15.chan_ref), custom_call_target="tpu_custom_call" | custom-call | tf_op jit(solution)/shard_map/reduce_grads/pallas_call | solution.py:445
  117.8 0.0 copy-start.1
  117.8 1.7 %copy.18 = f32[4,64,256]{2,1,0:T(8,128)} copy(f32[4,64,256]{2,1,0:T(8,128)} %get-tuple-element.32) | data formatting | bytes 524288
  119.5 0.0 copy-done.1
  119.5 0.7 copy.19
  (2 shorter events, 0.0 us)
Async XLA Ops:
  2.1 9.1 %copy-start = (bf16[1,512,4,256]{3,2,1,0:T(4,128)(2,1)S(1)}, bf16[1,512,4,256]{3,2,1,0:T(4,128)(2,1)}, u32[]{:S(2)}) copy-start(bf16[1,512,4,256]{3,2,1,0:T(4,128)(2,1)} %param.6) | copy-start | bytes 3145732
  117.8 1.7 %copy-start.1 = (f32[4,64,256]{2,1,0:T(8,128)S(1)}, f32[4,64,256]{2,1,0:T(8,128)}, u32[]{:S(2)}) copy-start(f32[4,64,256]{2,1,0:T(8,128)} %get-tuple-element.33) | copy-start | bytes 786436
